TPU v7x, 32 devices: a whole 2x2x4 slice. The times are simulated.
32 devices in a mesh: groups: 2 (over y), section: 2 (over core), sp: 4 (over z), blk: 2 (over x).
Axes of the slice: x: 2, y: 2, z: 4, core: 2. Of those that a mesh axis runs over, the one named last changes fastest.
Arguments:
- latent: float32 [2, 12, 64, 128], P('section', ('groups', 'blk'), 'sp'), parts along dimension 1, may hold values from -6 to 6
- queries: bfloat16 [2, 12, 2, 128, 4096], P('section', ('groups', 'blk'), None, 'sp'), parts along dimension 1
- keys: bfloat16 [2, 12, 2, 128, 4096], P('section', ('groups', 'blk'), None, 'sp'), parts along dimension 1
- values: bfloat16 [2, 12, 2, 128, 4096], P('section', ('groups', 'blk'), None, 'sp'), parts along dimension 1, may hold values from -6 to 6
- head_weight: bfloat16 [2, 64, 4096], P('section'), may hold values from -5 to 5
- step_index: int32 [2, 12], P('section', ('groups', 'blk')), parts along dimension 1, may hold values from 0 to 39, as said below
- skip_flags: int32 [12], P(('groups', 'blk')), parts along dimension 0, may hold values 0 or 1
Outputs:
- velocity: float32 [2, 12, 64, 128], P('section', ('groups', 'blk'), 'sp'), parts along dimension 1
- next_latent: float32 [2, 12, 64, 128], P('section', ('groups', 'blk'), 'sp'), parts along dimension 1
There are 2 independent parts, one for each index of `groups`. A program takes and returns all parts, laid end to end along the dimension named above; an argument that names none is the same for every part. Nothing has to cross between parts.
Inputs may be any that keep to these rules, and one draw needn't show every extreme that they name: `step_index`: row 0 (high-noise section) lies below 25, some videos at 24; row 1 (low-noise section) lies in 25 to 39.
All inputs are finite; a program needn't handle non-finite values. No bound on the sum of `skip_flags` on one device may be relied on, other than what follows from the above.
Results may differ from a plain program's by a relative error of at most 0.0041.
Values may be sent and summed in bfloat16 or wider, within the bound.
No kernel may reach another device: no remote copies, remote signals or barrier semaphores. Data moves between devices by JAX's collectives and lax.ppermute only.
A program may use at most 64 MiB of HBM per device.

v0:
```python
import jax
import jax.numpy as jnp
from jax import lax
from jax.sharding import PartitionSpec as P

HD = 128
CH = 64
STEPS = 40
SWITCH = 25
noise_shift = 12.0
high_guidance = 4.0
low_guidance = 3.0


def shifted(array, axis, by):
    devices = lax.axis_size(axis)
    pairs = [(i, i + by) for i in range(devices) if 0 <= i + by < devices]
    return lax.ppermute(array, axis, pairs)


def noise_level(step_now):
    fraction = 1.0 - step_now.astype(jnp.float32) / STEPS
    return noise_shift * fraction / (1.0 + (noise_shift - 1.0) * fraction)


def attend_heads(query_part, key_part, value_part):
    item_count, length, feature_width = query_part.shape
    head_count = feature_width // HD
    query_view = query_part.reshape(item_count, length, head_count, HD)
    key_view = key_part.reshape(item_count, length, head_count, HD)
    value_view = value_part.reshape(item_count, length, head_count, HD)
    scores = jnp.einsum(
        "iqhd,ikhd->ihqk", query_view, key_view, preferred_element_type=jnp.float32
    ) * HD ** (-0.5)
    row_max = jnp.max(scores, axis=3, keepdims=True)
    exponent = jnp.exp(scores - row_max)
    row_total = jnp.sum(exponent, axis=3, keepdims=True)
    weights = (exponent / row_total).astype(jnp.bfloat16)
    attended = jnp.einsum(
        "ihqk,ikhd->iqhd", weights, value_view, preferred_element_type=jnp.float32
    ).astype(jnp.bfloat16)
    return attended.reshape(item_count, length, feature_width)


def on_device(latent, queries, keys, values, head_weight, step_index, skip_flags):
    section_index = lax.axis_index("section")
    video_count = queries.shape[1]
    token_rows = queries.shape[3]
    feature_all = queries.shape[4]
    items = video_count * 2
    query_local = queries[0].reshape(items, token_rows, feature_all)
    key_local = keys[0].reshape(items, token_rows, feature_all)
    value_local = values[0].reshape(items, token_rows, feature_all)
    weight_local = head_weight[0]
    attended = attend_heads(
        lax.all_to_all(query_local, "sp", split_axis=2, concat_axis=1, tiled=True),
        lax.all_to_all(key_local, "sp", split_axis=2, concat_axis=1, tiled=True),
        lax.all_to_all(value_local, "sp", split_axis=2, concat_axis=1, tiled=True),
    )
    item_count = attended.shape[0]
    returned = lax.all_to_all(attended, "sp", split_axis=1, concat_axis=2, tiled=True)
    projected = lax.dot_general(
        returned, weight_local, (((2,), (1,)), ((), ())), preferred_element_type=jnp.float32
    )
    exchanged = projected.reshape(item_count, token_rows // 2, 2 * CH)
    pass_velocity = exchanged.reshape(video_count, 2, token_rows // 2, 2 * CH)
    conditional = pass_velocity[:, 0]
    unconditional = pass_velocity[:, 1]
    guidance = jnp.where(section_index == 0, jnp.float32(high_guidance), jnp.float32(low_guidance))
    guided = unconditional + guidance * (conditional - unconditional)
    skipping = (section_index == 1) & (skip_flags == 1)
    guided = jnp.where(skipping[:, None, None], conditional, guided)
    step_now = step_index[0]
    step_size = noise_level(step_now + 1) - noise_level(step_now)
    updated = latent[0] + step_size[:, None, None] * guided
    finish_mark = jnp.where(
        (section_index == 0) & (step_now + 1 == SWITCH), jnp.float32(1.0), jnp.float32(0.0)
    )
    arrived, arrived_mark = shifted((updated, finish_mark), "section", 1)
    taking = (section_index == 1) & (arrived_mark > 0.5)
    next_latent = jnp.where(taking[:, None, None], arrived, updated)
    return (guided[None], next_latent[None])


def solution(mesh):
    placed = (
        P("section", ("groups", "blk"), "sp", None),
        P("section", ("groups", "blk"), None, "sp", None),
        P("section", ("groups", "blk"), None, "sp", None),
        P("section", ("groups", "blk"), None, "sp", None),
        P("section", None, None),
        P("section", ("groups", "blk")),
        P(("groups", "blk")),
    )
    return jax.shard_map(
        on_device,
        mesh=mesh,
        in_specs=placed,
        out_specs=(
            P("section", ("groups", "blk"), "sp", None),
            P("section", ("groups", "blk"), "sp", None),
        ),
        check_vma=False,
    )
```

profile of v0, /device:TPU:0, one launch (start us, length us, event | category | flops | bytes accessed | tf_op | source)
XLA Modules:
  0.0 233.9 jit_solution(9079173877737753087)
XLA Ops:
  0.6 0.0 copy-start
  0.6 8.5 %copy.51 = bf16[6,32,4096]{1,0,2:T(8,128)(2,1)} copy(bf16[6,32,4096]{2,1,0:T(8,128)(2,1)} %bitcast.96) | data formatting | bytes 3145728 | tf_op jit(solution)/shard_map/reshape;squeeze | solution.py:51
  9.1 8.7 %reshape.125 = bf16[4,2,98304]{2,1,0:T(2,128)(2,1)} reshape(bf16[4096,6,32]{2,1,0:T(8,128)(2,1)} %bitcast.84) | data formatting | bytes 3145728
  17.9 6.3 %all-to-all-start = ((bf16[4,2,98304]{2,1,0:T(2,128)(2,1)}), bf16[4,2,98304]{2,1,0:T(2,128)(2,1)S(1)}, u32[]{:S(2)}, u32[]{:S(2)}) async-start(bf16[4,2,98304]{2,1,0:T(2,128)(2,1)} %reshape.125), calls=%async_computation | async-start | bytes 3145728 | tf_op jit(solution)/shard_map/all_to_all | solution.py:56
  24.2 8.4 %copy.54 = bf16[6,32,4096]{1,0,2:T(8,128)(2,1)} copy(bf16[6,32,4096]{2,1,0:T(8,128)(2,1)} %bitcast.97) | data formatting | bytes 3145728 | tf_op jit(solution)/shard_map/reshape;squeeze | solution.py:52
  32.6 8.7 %reshape.123 = bf16[4,2,98304]{2,1,0:T(2,128)(2,1)} reshape(bf16[4096,6,32]{2,1,0:T(8,128)(2,1)} %bitcast.85) | data formatting | bytes 3145728
  41.3 19.8 %all-to-all-done = bf16[4,2,98304]{2,1,0:T(2,128)(2,1)S(1)} async-done(((bf16[4,2,98304]{2,1,0:T(2,128)(2,1)}), bf16[4,2,98304]{2,1,0:T(2,128)(2,1)S(1)}, u32[]{:S(2)}, u32[]{:S(2)}) %all-to-all-start) | async-done | bytes 1572896 | tf_op jit(solution)/shard_map/all_to_all | solution.py:56
  61.1 0.0 copy-start.1
  61.1 1.2 copy-done.1
  62.3 4.4 %all-to-all-start.1 = ((bf16[4,2,98304]{2,1,0:T(2,128)(2,1)}), bf16[4,2,98304]{2,1,0:T(2,128)(2,1)}, u32[]{:S(2)}, u32[]{:S(2)}) async-start(bf16[4,2,98304]{2,1,0:T(2,128)(2,1)} %reshape.123), calls=%async_computation.1 | async-start | bytes 3145728 | tf_op jit(solution)/shard_map/all_to_all | solution.py:57
  66.7 8.4 %copy.59 = bf16[6,32,4096]{1,0,2:T(8,128)(2,1)} copy(bf16[6,32,4096]{2,1,0:T(8,128)(2,1)} %bitcast.98) | data formatting | bytes 3145728 | tf_op jit(solution)/shard_map/reshape;squeeze | solution.py:53
  75.1 8.8 %reshape.127 = bf16[4,2,98304]{2,1,0:T(2,128)(2,1)} reshape(bf16[4096,6,32]{2,1,0:T(8,128)(2,1)} %bitcast.86) | data formatting | bytes 3145728
  83.8 19.4 %all-to-all-done.1 = bf16[4,2,98304]{2,1,0:T(2,128)(2,1)} async-done(((bf16[4,2,98304]{2,1,0:T(2,128)(2,1)}), bf16[4,2,98304]{2,1,0:T(2,128)(2,1)}, u32[]{:S(2)}, u32[]{:S(2)}) %all-to-all-start.1) | async-done | bytes 1572896 | tf_op jit(solution)/shard_map/all_to_all | solution.py:57
  103.2 3.7 %all-to-all-start.2 = ((bf16[4,2,98304]{2,1,0:T(2,128)(2,1)}), bf16[4,2,98304]{2,1,0:T(2,128)(2,1)S(1)}, u32[]{:S(2)}, u32[]{:S(2)}) async-start(bf16[4,2,98304]{2,1,0:T(2,128)(2,1)} %reshape.127), calls=%async_computation.2 | async-start | bytes 3145728 | tf_op jit(solution)/shard_map/all_to_all | solution.py:58
  106.9 7.9 %reshape.126 = bf16[4096,6,32]{2,1,0:T(8,128)(2,1)} reshape(bf16[4,2,98304]{2,1,0:T(2,128)(2,1)} %copy-done.1) | data formatting | bytes 3145728
  114.8 9.1 %copy.70 = bf16[6,32,4,1024]{3,2,1,0:T(4,128)(2,1)} copy(bf16[6,32,4,1024]{1,0,3,2:T(8,128)(2,1)} %bitcast.81) | data formatting | bytes 3145728 | tf_op jit(solution)/shard_map/all_to_all | solution.py:56
  123.9 1.9 copy.53
  125.8 1.6 copy.77
  127.4 7.9 %reshape.124 = bf16[4096,6,32]{2,1,0:T(8,128)(2,1)} reshape(bf16[4,2,98304]{2,1,0:T(2,128)(2,1)} %all-to-all-done.1) | data formatting | bytes 3145728
  135.3 9.1 %copy.71 = bf16[6,32,4,1024]{3,2,1,0:T(4,128)(2,1)} copy(bf16[6,32,4,1024]{1,0,3,2:T(8,128)(2,1)} %bitcast.82) | data formatting | bytes 3145728 | tf_op jit(solution)/shard_map/all_to_all | solution.py:57
  144.4 1.9 copy.56
  146.3 0.0 copy-start.2
  146.3 0.4 copy.78
  146.8 1.0 copy-done.2
  147.7 1.2 fusion.5
  148.9 2.5 %fusion.20 = (f32[6,8,128]{2,1,0:T(8,128)S(1)}, f32[6,8,128,128]{2,3,1,0:T(8,128)}) fusion(f32[6,8,128,128]{2,3,1,0:T(8,128)S(1)} %fusion.5), kind=kOutput, calls=%fused_computation.31 | output fusion | flops 3145855 | bytes 6316032 | tf_op jit(solution)/shard_map/sub | solution.py:36
  151.4 0.0 all-to-all-done.2
  151.4 6.9 %reshape.128 = bf16[4096,6,32]{2,1,0:T(8,128)(2,1)} reshape(bf16[4,2,98304]{2,1,0:T(2,128)(2,1)S(1)} %all-to-all-done.2) | data formatting | bytes 3145728
  158.4 8.4 %copy.72 = bf16[6,32,4,1024]{3,2,1,0:T(4,128)(2,1)S(1)} copy(bf16[6,32,4,1024]{1,0,3,2:T(8,128)(2,1)} %bitcast.83) | data formatting | bytes 3145728 | tf_op jit(solution)/shard_map/all_to_all | solution.py:58
  166.8 0.5 copy.61
  167.3 0.0 copy-start.3
  167.3 0.4 copy.76
  167.8 1.4 copy-done.3
  169.2 0.7 convolution_convert_fusion
  169.9 3.0 %copy.64 = bf16[6,128,1024]{2,0,1:T(8,128)(2,1)} copy(bf16[6,128,1024]{1,2,0:T(8,128)(2,1)S(1)} %bitcast.99) | data formatting | bytes 3145728 | tf_op jit(solution)/shard_map/reshape | solution.py:42
  172.9 0.0 copy-start.5
  172.9 0.0 copy-start.6
  172.9 5.0 %all-to-all-start.3 = ((bf16[6,128,1024]{2,0,1:T(8,128)(2,1)}), bf16[6,128,1024]{2,0,1:T(8,128)(2,1)S(1)}, u32[]{:S(2)}, u32[]{:S(2)}) async-start(bf16[6,128,1024]{2,0,1:T(8,128)(2,1)} %copy.64), calls=%async_computation.3 | async-start | bytes 4194304 | tf_op jit(solution)/shard_map/all_to_all | solution.py:61
  177.9 0.0 copy-done.5
  177.9 1.3 collective-permute-start
  179.2 0.0 copy-done.6
  179.2 0.8 collective-permute-done
  180.0 45.0 %all-to-all-done.3 = bf16[6,128,1024]{2,0,1:T(8,128)(2,1)S(1)} async-done(((bf16[6,128,1024]{2,0,1:T(8,128)(2,1)}), bf16[6,128,1024]{2,0,1:T(8,128)(2,1)S(1)}, u32[]{:S(2)}, u32[]{:S(2)}) %all-to-all-start.3) | async-done | bytes 1572896 | tf_op jit(solution)/shard_map/all_to_all | solution.py:61
  225.0 2.4 %copy.66 = bf16[6,32,4,1024]{3,2,1,0:T(4,128)(2,1)} copy(bf16[6,32,4,1024]{3,0,1,2:T(8,128)(2,1)S(1)} %bitcast.87) | data formatting | bytes 3145728 | tf_op jit(solution)/shard_map/all_to_all | solution.py:61
  227.4 2.8 %all_to_all.58 = bf16[6,32,4096]{2,1,0:T(8,128)(2,1)S(1)} reshape(bf16[6,32,4,1024]{3,2,1,0:T(4,128)(2,1)} %copy.66) | data formatting | bytes 3145728 | tf_op jit(solution)/shard_map/all_to_all | solution.py:61
  230.3 0.0 copy-done
  230.3 0.0 copy-start.4
  230.3 0.6 fusion.10
  230.8 0.1 reshape_reshape.3
  230.9 0.1 copy-done.4
  231.0 0.1 fusion.15
  231.1 1.3 collective-permute-start.1
  232.4 0.7 fusion.17
  233.1 0.1 collective-permute-done.1
  233.2 0.7 select_bitcast_fusion
  (3 shorter events, 0.0 us)
Async XLA Ops:
  0.6 229.6 %copy-start = (bf16[1,64,4096]{2,1,0:T(8,128)(2,1)S(1)}, bf16[1,64,4096]{2,1,0:T(8,128)(2,1)}, u32[]{:S(2)}) copy-start(bf16[1,64,4096]{2,1,0:T(8,128)(2,1)} %param.11) | copy-start | bytes 1572868
  17.9 43.3 %all-to-all-start = ((bf16[4,2,98304]{2,1,0:T(2,128)(2,1)}), bf16[4,2,98304]{2,1,0:T(2,128)(2,1)S(1)}, u32[]{:S(2)}, u32[]{:S(2)}) async-start(bf16[4,2,98304]{2,1,0:T(2,128)(2,1)} %reshape.125), calls=%async_computation | async-start | bytes 3145728 | tf_op jit(solution)/shard_map/all_to_all | solution.py:56
  61.1 1.2 copy-start.1
  62.3 40.9 %all-to-all-start.1 = ((bf16[4,2,98304]{2,1,0:T(2,128)(2,1)}), bf16[4,2,98304]{2,1,0:T(2,128)(2,1)}, u32[]{:S(2)}, u32[]{:S(2)}) async-start(bf16[4,2,98304]{2,1,0:T(2,128)(2,1)} %reshape.123), calls=%async_computation.1 | async-start | bytes 3145728 | tf_op jit(solution)/shard_map/all_to_all | solution.py:57
  103.2 48.2 %all-to-all-start.2 = ((bf16[4,2,98304]{2,1,0:T(2,128)(2,1)}), bf16[4,2,98304]{2,1,0:T(2,128)(2,1)S(1)}, u32[]{:S(2)}, u32[]{:S(2)}) async-start(bf16[4,2,98304]{2,1,0:T(2,128)(2,1)} %reshape.127), calls=%async_computation.2 | async-start | bytes 3145728 | tf_op jit(solution)/shard_map/all_to_all | solution.py:58
  146.3 1.4 copy-start.2
  167.3 1.9 copy-start.3
  172.9 5.0 %copy-start.5 = (s32[1,3]{1,0:T(1,128)S(1)}, s32[1,3]{1,0:T(1,128)}, u32[]{:S(2)}) copy-start(s32[1,3]{1,0:T(1,128)} %param.12) | copy-start | bytes 40
  172.9 6.3 %copy-start.6 = (s32[3]{0:T(128)S(1)}, s32[3]{0:T(128)}, u32[]{:S(2)}) copy-start(s32[3]{0:T(128)} %param.13) | copy-start | bytes 40
  172.9 52.1 %all-to-all-start.3 = ((bf16[6,128,1024]{2,0,1:T(8,128)(2,1)}), bf16[6,128,1024]{2,0,1:T(8,128)(2,1)S(1)}, u32[]{:S(2)}, u32[]{:S(2)}) async-start(bf16[6,128,1024]{2,0,1:T(8,128)(2,1)} %copy.64), calls=%async_computation.3 | async-start | bytes 4194304 | tf_op jit(solution)/shard_map/all_to_all | solution.py:61
  177.9 2.1 collective-permute-start
  230.3 0.7 copy-start.4
  231.1 2.1 collective-permute-start.1
where the time goes:
time: 236 us; the launch traced here: 234 us
  local copies, waits for them, and re-layouts  120 us (51%)
  waiting for transfers between devices  85.1 us (36%)
  starting transfers between devices  22 us (9%)
  other arithmetic  3.95 us (2%)
  matrix products  2.45 us (1%)
    unnamed x23, local copies, waits for them, and re-layouts  55 us
    all_to_all x1, waiting for transfers between devices, on_device(): lax.all_to_all(attended, 'sp', split_axis=1, concat_axis=2, tiled=True)  45 us
    all_to_all x1, waiting for transfers between devices, on_device(): lax.all_to_all(query_local, 'sp', split_axis=2, concat_axis=1, tiled=True)  19.8 us
    all_to_all x1, waiting for transfers between devices, on_device(): lax.all_to_all(key_local, 'sp', split_axis=2, concat_axis=1, tiled=True)  19.4 us
    all_to_all x2, local copies, waits for them, and re-layouts, on_device(): lax.all_to_all(key_local, 'sp', split_axis=2, concat_axis=1, tiled=True)  11 us
    all_to_all x2, local copies, waits for them, and re-layouts, on_device(): lax.all_to_all(query_local, 'sp', split_axis=2, concat_axis=1, tiled=True)  11 us
    all_to_all x2, local copies, waits for them, and re-layouts, on_device(): lax.all_to_all(value_local, 'sp', split_axis=2, concat_axis=1, tiled=True)  8.94 us
    another operation x1, local copies, waits for them, and re-layouts, on_device(): query_local = queries[0].reshape(items, token_rows, feature_all)  8.47 us
  transfers between devices with their start and end apart: 6, of which 5 were waited for; matrix products, arithmetic and copies ran while one was open for 34% of the time, Pallas kernels for 0%

commit v1 on v0

--- a/solution.py
+++ b/solution.py
@@ -55,7 +55,12 @@
     attended = attend_heads(
         lax.all_to_all(query_local, "sp", split_axis=2, concat_axis=1, tiled=True),
         lax.all_to_all(key_local, "sp", split_axis=2, concat_axis=1, tiled=True),
-        lax.all_to_all(value_local, "sp", split_axis=2, concat_axis=1, tiled=True),
+        jnp.concatenate(
+            lax.all_to_all(
+                jnp.stack(jnp.split(value_local, lax.axis_size("sp"), axis=2)), "sp", 0, 0
+            ),
+            axis=1,
+        ),
     )
     item_count = attended.shape[0]
     returned = lax.all_to_all(attended, "sp", split_axis=1, concat_axis=2, tiled=True)

time: 236 us -> 215 us (0.911)
  local copies, waits for them, and re-layouts: 120 us -> 83.3 us
  waiting for transfers between devices: 85.1 us -> 99.4 us
    unnamed x23 -> x19, local copies, waits for them, and re-layouts: 55 us -> 37.3 us
    all_to_all x1, waiting for transfers between devices: 19.8 us -> 33.6 us  [on_device(): lax.all_to_all(query_local, 'sp', split_axis=2, concat_axis=1, tiled=True)]
    all_to_all x2 -> x0, local copies, waits for them, and re-layouts: 8.94 us -> none  [on_device(): lax.all_to_all(value_local, 'sp', split_axis=2, concat_axis=1, tiled=True)]
    another operation x1, local copies, waits for them, and re-layouts: 8.42 us -> 1.51 us  [on_device(): jnp.stack(jnp.split(value_local, lax.axis_size('sp'), axis=2))]
  transfers between devices with their start and end apart: 6 -> 6, of which waited for: 5 -> 5; matrix products, arithmetic and copies ran while one was open for 34% -> 28% of each run, Pallas kernels for 0% -> 0%
where the time goes in v1:
time: 215 us; the launch traced here: 214 us
  waiting for transfers between devices  99.4 us (46%)
  local copies, waits for them, and re-layouts  83.3 us (39%)
  starting transfers between devices  22.7 us (11%)
  other arithmetic  5.28 us (2%)
  matrix products  2.45 us (1%)
    all_to_all x1, waiting for transfers between devices, on_device(): lax.all_to_all(attended, 'sp', split_axis=1, concat_axis=2, tiled=True)  45 us
    unnamed x19, local copies, waits for them, and re-layouts  37.3 us
    all_to_all x1, waiting for transfers between devices, on_device(): lax.all_to_all(query_local, 'sp', split_axis=2, concat_axis=1, tiled=True)  33.6 us
    all_to_all x1, waiting for transfers between devices, on_device(): lax.all_to_all(key_local, 'sp', split_axis=2, concat_axis=1, tiled=True)  19.8 us
    all_to_all x2, local copies, waits for them, and re-layouts, on_device(): lax.all_to_all(query_local, 'sp', split_axis=2, concat_axis=1, tiled=True)  8.94 us
    all_to_all x2, local copies, waits for them, and re-layouts, on_device(): lax.all_to_all(key_local, 'sp', split_axis=2, concat_axis=1, tiled=True)  8.94 us
    another operation x1, local copies, waits for them, and re-layouts, on_device(): key_local = keys[0].reshape(items, token_rows, feature_all)  8.47 us
    another operation x1, local copies, waits for them, and re-layouts, on_device(): query_local = queries[0].reshape(items, token_rows, feature_all)  8.41 us
  transfers between devices with their start and end apart: 6, of which 5 were waited for; matrix products, arithmetic and copies ran while one was open for 28% of the time, Pallas kernels for 0%

profile of v1, /device:TPU:0, one launch (start us, length us, event | category | flops | bytes accessed | tf_op | source)
XLA Modules:
  0.0 214.0 jit_solution(7060356717316631545)
XLA Ops:
  0.6 0.0 copy-start
  0.6 8.5 %copy.57 = bf16[6,32,4096]{1,0,2:T(8,128)(2,1)} copy(bf16[6,32,4096]{2,1,0:T(8,128)(2,1)} %bitcast.98) | data formatting | bytes 3145728 | tf_op jit(solution)/shard_map/reshape;squeeze | solution.py:52
  9.1 8.7 %reshape.122 = bf16[4,2,98304]{2,1,0:T(2,128)(2,1)} reshape(bf16[4096,6,32]{2,1,0:T(8,128)(2,1)} %bitcast.88) | data formatting | bytes 3145728
  17.9 6.3 %all-to-all-start.2 = ((bf16[4,2,98304]{2,1,0:T(2,128)(2,1)}), bf16[4,2,98304]{2,1,0:T(2,128)(2,1)S(1)}, u32[]{:S(2)}, u32[]{:S(2)}) async-start(bf16[4,2,98304]{2,1,0:T(2,128)(2,1)} %reshape.122), calls=%async_computation.2 | async-start | bytes 3145728 | tf_op jit(solution)/shard_map/all_to_all | solution.py:57
  24.2 8.4 %copy.54 = bf16[6,32,4096]{1,0,2:T(8,128)(2,1)} copy(bf16[6,32,4096]{2,1,0:T(8,128)(2,1)} %bitcast.99) | data formatting | bytes 3145728 | tf_op jit(solution)/shard_map/reshape;squeeze | solution.py:51
  32.6 8.7 %reshape.124 = bf16[4,2,98304]{2,1,0:T(2,128)(2,1)} reshape(bf16[4096,6,32]{2,1,0:T(8,128)(2,1)} %bitcast.89) | data formatting | bytes 3145728
  41.3 19.8 %all-to-all-done.2 = bf16[4,2,98304]{2,1,0:T(2,128)(2,1)S(1)} async-done(((bf16[4,2,98304]{2,1,0:T(2,128)(2,1)}), bf16[4,2,98304]{2,1,0:T(2,128)(2,1)S(1)}, u32[]{:S(2)}, u32[]{:S(2)}) %all-to-all-start.2) | async-done | bytes 1572896 | tf_op jit(solution)/shard_map/all_to_all | solution.py:57
  61.1 4.3 %all-to-all-start.1 = ((bf16[4,2,98304]{2,1,0:T(2,128)(2,1)}), bf16[4,2,98304]{2,1,0:T(2,128)(2,1)}, u32[]{:S(2)}, u32[]{:S(2)}) async-start(bf16[4,2,98304]{2,1,0:T(2,128)(2,1)} %reshape.124), calls=%async_computation.1 | async-start | bytes 3145728 | tf_op jit(solution)/shard_map/all_to_all | solution.py:56
  65.5 1.5 slice_bitcast_fusion.3
  67.0 1.4 pad_maximum_fusion
  68.4 33.6 %all-to-all-done.1 = bf16[4,2,98304]{2,1,0:T(2,128)(2,1)} async-done(((bf16[4,2,98304]{2,1,0:T(2,128)(2,1)}), bf16[4,2,98304]{2,1,0:T(2,128)(2,1)}, u32[]{:S(2)}, u32[]{:S(2)}) %all-to-all-start.1) | async-done | bytes 1572896 | tf_op jit(solution)/shard_map/all_to_all | solution.py:56
  102.0 4.5 %all-to-all-start = ((bf16[4,6,32,1024]{3,2,1,0:T(8,128)(2,1)}), bf16[4,6,32,1024]{3,2,1,0:T(8,128)(2,1)}, u32[]{:S(2)}, u32[]{:S(2)}) async-start(bf16[4,6,32,1024]{3,2,1,0:T(8,128)(2,1)} %pad_maximum_fusion), calls=%async_computation | async-start | bytes 3145728 | tf_op jit(solution)/shard_map/all_to_all | solution.py:59
  106.5 7.0 %reshape.123 = bf16[4096,6,32]{2,1,0:T(8,128)(2,1)} reshape(bf16[4,2,98304]{2,1,0:T(2,128)(2,1)S(1)} %all-to-all-done.2) | data formatting | bytes 3145728
  113.5 8.4 %copy.71 = bf16[6,32,4,1024]{3,2,1,0:T(4,128)(2,1)S(1)} copy(bf16[6,32,4,1024]{1,0,3,2:T(8,128)(2,1)} %bitcast.86) | data formatting | bytes 3145728 | tf_op jit(solution)/shard_map/all_to_all | solution.py:57
  121.9 0.5 copy.59
  122.4 1.6 copy.77
  124.1 7.9 %reshape.125 = bf16[4096,6,32]{2,1,0:T(8,128)(2,1)} reshape(bf16[4,2,98304]{2,1,0:T(2,128)(2,1)} %all-to-all-done.1) | data formatting | bytes 3145728
  131.9 8.4 %copy.70 = bf16[6,32,4,1024]{3,2,1,0:T(4,128)(2,1)S(1)} copy(bf16[6,32,4,1024]{1,0,3,2:T(8,128)(2,1)} %bitcast.87) | data formatting | bytes 3145728 | tf_op jit(solution)/shard_map/all_to_all | solution.py:56
  140.4 0.5 copy.56
  140.9 0.0 copy-start.1
  140.9 0.4 copy.76
  141.3 1.0 copy-done.1
  142.3 1.2 fusion.5
  143.5 2.4 %fusion.20 = (f32[6,8,128]{2,1,0:T(8,128)S(1)}, f32[6,8,128,128]{2,3,1,0:T(8,128)}) fusion(f32[6,8,128,128]{2,3,1,0:T(8,128)S(1)} %fusion.5), kind=kOutput, calls=%fused_computation.36 | output fusion | flops 3145855 | bytes 6316032 | tf_op jit(solution)/shard_map/sub | solution.py:36
  145.9 0.0 all-to-all-done
  145.9 1.6 copy.53
  147.5 0.0 copy-start.2
  147.5 0.4 copy.75
  147.9 1.4 copy-done.2
  149.4 0.7 convolution_convert_fusion
  150.1 3.0 %copy.64 = bf16[6,128,1024]{2,0,1:T(8,128)(2,1)} copy(bf16[6,128,1024]{1,2,0:T(8,128)(2,1)S(1)} %bitcast.100) | data formatting | bytes 3145728 | tf_op jit(solution)/shard_map/reshape | solution.py:42
  153.0 0.0 copy-start.4
  153.0 0.0 copy-start.5
  153.0 5.0 %all-to-all-start.3 = ((bf16[6,128,1024]{2,0,1:T(8,128)(2,1)}), bf16[6,128,1024]{2,0,1:T(8,128)(2,1)S(1)}, u32[]{:S(2)}, u32[]{:S(2)}) async-start(bf16[6,128,1024]{2,0,1:T(8,128)(2,1)} %copy.64), calls=%async_computation.3 | async-start | bytes 4194304 | tf_op jit(solution)/shard_map/all_to_all | solution.py:66
  158.0 0.0 copy-done.4
  158.0 1.3 collective-permute-start
  159.3 0.0 copy-done.5
  159.3 0.8 collective-permute-done
  160.1 45.0 %all-to-all-done.3 = bf16[6,128,1024]{2,0,1:T(8,128)(2,1)S(1)} async-done(((bf16[6,128,1024]{2,0,1:T(8,128)(2,1)}), bf16[6,128,1024]{2,0,1:T(8,128)(2,1)S(1)}, u32[]{:S(2)}, u32[]{:S(2)}) %all-to-all-start.3) | async-done | bytes 1572896 | tf_op jit(solution)/shard_map/all_to_all | solution.py:66
  205.1 2.4 %copy.66 = bf16[6,32,4,1024]{3,2,1,0:T(4,128)(2,1)} copy(bf16[6,32,4,1024]{3,0,1,2:T(8,128)(2,1)S(1)} %bitcast.90) | data formatting | bytes 3145728 | tf_op jit(solution)/shard_map/all_to_all | solution.py:66
  207.5 2.8 %all_to_all.48 = bf16[6,32,4096]{2,1,0:T(8,128)(2,1)S(1)} reshape(bf16[6,32,4,1024]{3,2,1,0:T(4,128)(2,1)} %copy.66) | data formatting | bytes 3145728 | tf_op jit(solution)/shard_map/all_to_all | solution.py:66
  210.4 0.0 copy-done
  210.4 0.0 copy-start.3
  210.4 0.6 fusion.10
  210.9 0.1 reshape_reshape.7
  211.0 0.1 copy-done.3
  211.1 0.1 fusion.15
  211.2 1.3 collective-permute-start.1
  212.5 0.7 fusion.17
  213.2 0.1 collective-permute-done.1
  213.3 0.7 select_bitcast_fusion
  (3 shorter events, 0.0 us)
Async XLA Ops:
  0.6 209.7 %copy-start = (bf16[1,64,4096]{2,1,0:T(8,128)(2,1)S(1)}, bf16[1,64,4096]{2,1,0:T(8,128)(2,1)}, u32[]{:S(2)}) copy-start(bf16[1,64,4096]{2,1,0:T(8,128)(2,1)} %param.11) | copy-start | bytes 1572868
  17.9 43.3 %all-to-all-start.2 = ((bf16[4,2,98304]{2,1,0:T(2,128)(2,1)}), bf16[4,2,98304]{2,1,0:T(2,128)(2,1)S(1)}, u32[]{:S(2)}, u32[]{:S(2)}) async-start(bf16[4,2,98304]{2,1,0:T(2,128)(2,1)} %reshape.122), calls=%async_computation.2 | async-start | bytes 3145728 | tf_op jit(solution)/shard_map/all_to_all | solution.py:57
  61.1 40.9 %all-to-all-start.1 = ((bf16[4,2,98304]{2,1,0:T(2,128)(2,1)}), bf16[4,2,98304]{2,1,0:T(2,128)(2,1)}, u32[]{:S(2)}, u32[]{:S(2)}) async-start(bf16[4,2,98304]{2,1,0:T(2,128)(2,1)} %reshape.124), calls=%async_computation.1 | async-start | bytes 3145728 | tf_op jit(solution)/shard_map/all_to_all | solution.py:56
  102.0 43.9 %all-to-all-start = ((bf16[4,6,32,1024]{3,2,1,0:T(8,128)(2,1)}), bf16[4,6,32,1024]{3,2,1,0:T(8,128)(2,1)}, u32[]{:S(2)}, u32[]{:S(2)}) async-start(bf16[4,6,32,1024]{3,2,1,0:T(8,128)(2,1)} %pad_maximum_fusion), calls=%async_computation | async-start | bytes 3145728 | tf_op jit(solution)/shard_map/all_to_all | solution.py:59
  140.9 1.4 copy-start.1
  147.5 1.9 copy-start.2
  153.0 5.0 %copy-start.4 = (s32[1,3]{1,0:T(1,128)S(1)}, s32[1,3]{1,0:T(1,128)}, u32[]{:S(2)}) copy-start(s32[1,3]{1,0:T(1,128)} %param.12) | copy-start | bytes 40
  153.0 6.3 %copy-start.5 = (s32[3]{0:T(128)S(1)}, s32[3]{0:T(128)}, u32[]{:S(2)}) copy-start(s32[3]{0:T(128)} %param.13) | copy-start | bytes 40
  153.0 52.1 %all-to-all-start.3 = ((bf16[6,128,1024]{2,0,1:T(8,128)(2,1)}), bf16[6,128,1024]{2,0,1:T(8,128)(2,1)S(1)}, u32[]{:S(2)}, u32[]{:S(2)}) async-start(bf16[6,128,1024]{2,0,1:T(8,128)(2,1)} %copy.64), calls=%async_computation.3 | async-start | bytes 4194304 | tf_op jit(solution)/shard_map/all_to_all | solution.py:66
  158.0 2.1 collective-permute-start
  210.4 0.7 copy-start.3
  211.2 2.1 collective-permute-start.1
